TPU v7x, 32 devices: a whole 2x2x4 slice. The times are simulated.
32 devices in a mesh: rep: 4 (over z), fsdp: 8 (over y, x, core).
Axes of the slice: x: 2, y: 2, z: 4, core: 2. Of those that a mesh axis runs over, the one named last changes fastest.
Arguments:
- activations: bfloat16 [4, 16384, 4096], P('rep', 'fsdp'), may hold values from -6 to 6
- cotangent: bfloat16 [4, 16384, 1024], P('rep', 'fsdp'), may hold values from -0.046875 to 0.046875
- momentum: float32 [4, 4096, 1024], P('rep', 'fsdp'), may hold values from -6 to 6
Outputs:
- momentum_next: float32 [4, 4096, 1024], P('rep', 'fsdp')
- update: float32 [4096, 1024], P('fsdp')
All inputs are finite; a program needn't handle non-finite values.
Results may differ from a plain program's by a relative error of at most 0.0021.
Values sent between devices are 32-bit elements; how exact they have to be, the bound alone decides.
No kernel may reach another device: no remote copies, remote signals or barrier semaphores. Data moves between devices by JAX's collectives and lax.ppermute only.
A program may use at most 128 MiB of HBM per device.

v0:
```python
import jax
import jax.numpy as jnp
from jax import lax
from jax.sharding import PartitionSpec as P

CH = 64
BAND = 16
momentum_decay = 0.9


def basis_rows(size, keep):
    freq = jnp.arange(keep, dtype=jnp.float32)[:, None]
    point = jnp.arange(size, dtype=jnp.float32)[None, :]
    waves = jnp.cos(jnp.pi * (2.0 * point + 1.0) * freq / (2.0 * size))
    scales = jnp.where(freq == 0.0, jnp.sqrt(1.0 / size), jnp.sqrt(2.0 / size))
    return waves * scales


def bands_of(field, basis):
    rows, width = field.shape
    blocks = field.reshape(rows // CH, CH, width // CH, CH)
    return jnp.einsum("kn,anbm,lm->akbl", basis, blocks, basis, precision=lax.Precision.HIGHEST)


def term_maker(normed, part):
    return lax.dot_general(
        normed, part, (((0,), (0,)), ((), ())), preferred_element_type=jnp.float32
    )


def settle(grad, field, basis):
    accumulated = momentum_decay * field + grad
    bands = bands_of(accumulated, basis)
    count, _, wide, _ = bands.shape
    blocks = jnp.einsum("kn,akbl,lm->anbm", basis, bands, basis, precision=lax.Precision.HIGHEST)
    return (accumulated - blocks.reshape(count * CH, wide * CH), bands)


def body(activations, cotangent, momentum):
    values = activations[0].astype(jnp.float32)
    stat = jnp.mean(values * values, axis=-1, keepdims=True)
    normed = (values * lax.rsqrt(stat + 1e-05)).astype(jnp.bfloat16)
    targets = cotangent[0]
    field = momentum[0]
    basis = basis_rows(CH, BAND)
    grad = lax.psum_scatter(term_maker(normed, targets), "fsdp", scatter_dimension=0, tiled=True)
    cleared, bands = settle(grad, field, basis)
    count, _, wide, _ = bands.shape
    summed = lax.psum(bands, "rep")
    blocks = jnp.einsum("kn,akbl,lm->anbm", basis, summed, basis, precision=lax.Precision.HIGHEST)
    update = blocks.reshape(count * CH, wide * CH)
    groups = lax.axis_size("rep")
    return (cleared[None], update / groups)


def solution(mesh):
    return jax.shard_map(
        body,
        mesh=mesh,
        in_specs=(P("rep", "fsdp", None), P("rep", "fsdp", None), P("rep", "fsdp", None)),
        out_specs=(P("rep", "fsdp", None), P("fsdp", None)),
        check_vma=False,
    )
```

profile of v0, /device:TPU:0, one launch (start us, length us, event | category | flops | bytes accessed | tf_op | source)
XLA Modules:
  0.0 262.0 jit_solution(10249392141727543123)
XLA Ops:
  7.2 0.0 reduce-scatter.2.cloned.1.call-start
  7.2 0.0 copy-start
  7.2 7.6 %fusion = f32[2048]{0:T(1024)S(1)} fusion(bf16[1,2048,4096]{2,1,0:T(8,128)(2,1)} %param.3), kind=kLoop, calls=%fused_computation.2 | loop fusion | flops 25163776 | bytes 16785408 | tf_op jit(solution)/shard_map/reduce_sum | solution.py:41
  14.8 3.1 %copy-done = bf16[1,2048,4096]{2,1,0:T(8,128)(2,1)S(1)} copy-done((bf16[1,2048,4096]{2,1,0:T(8,128)(2,1)S(1)}, bf16[1,2048,4096]{2,1,0:T(8,128)(2,1)}, u32[]{:S(2)}) %copy-start) | copy-done | bytes 16777240
  17.9 23.4 %fusion.3 = f32[4096,1024]{1,0:T(8,128)} fusion(bf16[1,2048,4096]{2,1,0:T(8,128)(2,1)S(1)} %copy-done, f32[2048]{0:T(1024)S(1)} %add_rsqrt_fusion, bf16[1,2048,1024]{2,1,0:T(8,128)(2,1)} %param.4), kind=kOutput, calls=%fused_computation.5 | convolution fusion | flops 17205035008 | bytes 37756928 | tf_op jit(solution)/shard_map/dot_general | solution.py:26
  41.3 0.0 reduce-scatter.2.cloned.1.call-update
  41.3 119.0 %reduce-scatter.2.cloned.1.call-done = f32[512,1024]{1,0:T(8,128)} async-done(((f32[4096,1024]{1,0:T(8,128)}), f32[512,1024]{1,0:T(8,128)}) %reduce-scatter.2.cloned.1.call-update) | async-done | bytes 2097168 | tf_op jit(solution)/shard_map/reduce_scatter | solution.py:46
  160.3 2.7 %bitcast_add_fusion = f32[512,1024]{1,0:T(8,128)S(1)} fusion(f32[512,1024]{1,0:T(8,128)} %reduce-scatter.2.cloned.1.call-done, f32[1,512,1024]{2,1,0:T(8,128)} %param.5), kind=kLoop, calls=%fused_computation.12 | loop fusion | flops 1048576 | bytes 6291456 | tf_op jit(solution)/shard_map/add | solution.py:32
  163.0 2.5 reshape.49
  165.5 5.6 %fusion.7 = f32[8,16,64,16]{2,3,1,0:T(8,128)S(1)} fusion(f32[8,64,16,64]{3,2,1,0:T(8,128)} %reshape.49, f32[16]{0:T(128)S(1)} %compare_select_fusion, f32[64]{0:T(128)S(1)} %add_multiply_fusion), kind=kOutput, calls=%fused_computation.8 | convolution fusion | flops 100666368 | bytes 2621760 | tf_op jit(solution)/shard_map/kn,anbm,lm->akbl/dot_general | solution.py:22
  171.1 1.0 convolution_bitcast_fusion.1
  172.1 2.8 %fusion.13 = f32[8,16,16,64]{3,2,1,0:T(8,128)} fusion(f32[8,16,16,16]{3,1,2,0:T(8,128)S(1)} %convolution_bitcast_fusion.1, f32[16]{0:T(128)S(1)} %compare_select_fusion, f32[64]{0:T(128)S(1)} %add_multiply_fusion), kind=kOutput, calls=%fused_computation.19 | convolution fusion | flops 25168896 | bytes 655680 | tf_op jit(solution)/shard_map/kn,akbl,lm->anbm/dot_general | solution.py:35
  174.9 0.0 all-reduce.2.cloned.1.call-start
  174.9 9.3 %convolution_bitcast_fusion = f32[8,64,16,64]{3,1,2,0:T(8,128)} fusion(f32[8,16,16,64]{3,2,1,0:T(8,128)} %fusion.13, f32[16]{0:T(128)S(1)} %compare_select_fusion, f32[64]{0:T(128)S(1)} %add_multiply_fusion), kind=kOutput, calls=%fused_computation.11 | convolution fusion | flops 100666368 | bytes 2621760 | tf_op jit(solution)/shard_map/kn,akbl,lm->anbm/dot_general | solution.py:35
  184.2 0.0 copy-done.1
  184.2 0.0 all-reduce.2.cloned.1.call-update
  184.2 6.5 %copy.6 = f32[8,64,16,64]{3,2,1,0:T(8,128)} copy(f32[8,64,16,64]{3,1,2,0:T(8,128)} %convolution_bitcast_fusion) | data formatting | bytes 4194304 | tf_op jit(solution)/shard_map/kn,akbl,lm->anbm/transpose | solution.py:35
  190.8 4.8 %reshape.50 = f32[512,1024]{1,0:T(8,128)} reshape(f32[8,64,16,64]{3,2,1,0:T(8,128)} %copy.6) | data formatting | bytes 4194304 | tf_op jit(solution)/shard_map/reshape | solution.py:36
  195.6 3.3 %subtract_bitcast_fusion = f32[1,512,1024]{2,1,0:T(8,128)} fusion(f32[512,1024]{1,0:T(8,128)S(1)} %bitcast_add_fusion, f32[512,1024]{1,0:T(8,128)} %reshape.50), kind=kLoop, calls=%fused_computation.13 | loop fusion | flops 524288 | bytes 6291456 | tf_op jit(solution)/shard_map/broadcast_in_dim | solution.py:53
  198.9 37.4 %all-reduce.2.cloned.1.call-done = f32[8,16,16,16]{3,1,2,0:T(8,128)} async-done(((f32[8,16,16,16]{3,1,2,0:T(8,128)}), f32[8,16,16,16]{3,1,2,0:T(8,128)}) %all-reduce.2.cloned.1.call-update) | async-done | bytes 131088 | tf_op jit(solution)/shard_map/psum | solution.py:49
  236.3 3.0 %fusion.10 = f32[8,16,16,64]{3,2,1,0:T(8,128)S(1)} fusion(f32[8,16,16,16]{3,1,2,0:T(8,128)} %all-reduce.2.cloned.1.call-done, f32[16]{0:T(128)S(1)} %compare_select_fusion, f32[64]{0:T(128)S(1)} %add_multiply_fusion), kind=kOutput, calls=%fused_computation.16 | convolution fusion | flops 25168896 | bytes 655680 | tf_op jit(solution)/shard_map/kn,akbl,lm->anbm/dot_general | solution.py:50
  239.3 6.7 %multiply_bitcast_fusion = f32[8,64,16,64]{3,1,2,0:T(8,128)S(1)} fusion(f32[8,16,16,64]{3,2,1,0:T(8,128)S(1)} %fusion.10, f32[16]{0:T(128)S(1)} %compare_select_fusion, f32[64]{0:T(128)S(1)} %add_multiply_fusion), kind=kOutput, calls=%fused_computation.10 | convolution fusion | flops 101190656 | bytes 2621760 | tf_op jit(solution)/shard_map/kn,akbl,lm->anbm/dot_general | solution.py:50
  246.1 4.3 %copy.7 = f32[8,64,16,64]{3,2,1,0:T(8,128)} copy(f32[8,64,16,64]{3,1,2,0:T(8,128)S(1)} %multiply_bitcast_fusion) | data formatting | bytes 4194304 | tf_op jit(solution)/shard_map/div | solution.py:53
  250.4 4.8 %div.39 = f32[512,1024]{1,0:T(8,128)} reshape(f32[8,64,16,64]{3,2,1,0:T(8,128)} %copy.7) | data formatting | bytes 4194304 | tf_op jit(solution)/shard_map/div | solution.py:53
  (4 shorter events, 0.0 us)
Async XLA Ops:
  7.2 153.2 %reduce-scatter.2.cloned.1.call-start = ((), (), s32[]{:S(2)}) async-start(), calls=%async_computation.1 | async-start | bytes 18874368 | tf_op jit(solution)/shard_map/reduce_scatter | solution.py:46
  7.2 10.7 %copy-start = (bf16[1,2048,4096]{2,1,0:T(8,128)(2,1)S(1)}, bf16[1,2048,4096]{2,1,0:T(8,128)(2,1)}, u32[]{:S(2)}) copy-start(bf16[1,2048,4096]{2,1,0:T(8,128)(2,1)} %param.3) | copy-start | bytes 50331652
  172.1 12.1 %copy-start.1 = (f32[8,16,16,16]{3,1,2,0:T(8,128)}, f32[8,16,16,16]{3,1,2,0:T(8,128)S(1)}, u32[]{:S(2)}) copy-start(f32[8,16,16,16]{3,1,2,0:T(8,128)S(1)} %convolution_bitcast_fusion.1) | copy-start | bytes 393220
  174.9 61.4 %all-reduce.2.cloned.1.call-start = ((), (), s32[]{:S(2)}) async-start(), calls=%async_computation.2 | async-start | bytes 2097152 | tf_op jit(solution)/shard_map/psum | solution.py:49
Sparse Core Ops, SparseCore 0:
  41.4 118.8 reduce-scatter.1
  184.4 51.8 all-reduce.1
where the time goes:
time: 262 us
  waiting for transfers between devices  156 us (60%)
  matrix products  51.8 us (20%)
  local copies, waits for them, and re-layouts  26.1 us (10%)
  between operations  14.1 us (5%)
  other arithmetic  13.6 us (5%)
    reduce_scatter x1, waiting for transfers between devices, body(): lax.psum_scatter(term_maker(normed, targets), 'fsdp', scatter_dimension=0...  119 us
    psum x1, waiting for transfers between devices, body(): summed = lax.psum(bands, 'rep')  37.4 us
    dot_general x1, matrix products, term_maker(): lax.dot_general(normed, part, (((0,), (0,)), ((), ())), preferred_element...  23.4 us
    dot_general x2, matrix products, settle(): jnp.einsum('kn,akbl,lm->anbm', basis, bands, basis, precision=lax.Precisi...  12.1 us
    dot_general x2, matrix products, body(): jnp.einsum('kn,akbl,lm->anbm', basis, summed, basis, precision=lax.Precis...  9.76 us
    div x2, local copies, waits for them, and re-layouts, body(): return (cleared[None], update / groups)  9.14 us
    reduce_sum x1, other arithmetic, body(): stat = jnp.mean(values * values, axis=-1, keepdims=True)  7.6 us
    dot_general x2, matrix products, bands_of(): jnp.einsum('kn,anbm,lm->akbl', basis, blocks, basis, precision=lax.Precis...  6.6 us
  transfers between devices with their start and end apart: 2, of which 2 were waited for; matrix products, arithmetic and copies ran while one was open for 6% of the time, Pallas kernels for 0%

commit v1 on v0

--- a/solution.py
+++ b/solution.py
@@ -46,7 +46,9 @@
     grad = lax.psum_scatter(term_maker(normed, targets), "fsdp", scatter_dimension=0, tiled=True)
     cleared, bands = settle(grad, field, basis)
     count, _, wide, _ = bands.shape
-    summed = lax.psum(bands, "rep")
+    summed = bands
+    for hop in (1, 2):
+        summed = summed + lax.ppermute(summed, "rep", [(dev, dev ^ hop) for dev in range(4)])
     blocks = jnp.einsum("kn,akbl,lm->anbm", basis, summed, basis, precision=lax.Precision.HIGHEST)
     update = blocks.reshape(count * CH, wide * CH)
     groups = lax.axis_size("rep")

time: 262 us -> 273 us (1.042)
  waiting for transfers between devices: 156 us -> 170 us
  matrix products: 51.8 us -> 47.3 us
  starting transfers between devices: 0.04 us -> 4.04 us
    ppermute x0 -> x2, waiting for transfers between devices: none -> 50.7 us  [body(): lax.ppermute(summed, 'rep', [(dev, dev ^ hop) for dev in range(4)])]
    psum x1 -> x0, waiting for transfers between devices: 37.4 us -> none  [body(): summed = lax.psum(bands, 'rep')]
    ppermute x0 -> x2, starting transfers between devices: none -> 4 us  [body(): lax.ppermute(summed, 'rep', [(dev, dev ^ hop) for dev in range(4)])]
    dot_general x2, matrix products: 12.1 us -> 8.54 us  [settle(): jnp.einsum('kn,akbl,lm->anbm', basis, bands, basis, precision=lax.Precisi...]
  transfers between devices with their start and end apart: 2 -> 3, of which waited for: 2 -> 3; matrix products, arithmetic and copies ran while one was open for 6% -> 6% of each run, Pallas kernels for 0% -> 0%
where the time goes in v1:
time: 273 us; the launch traced here: 272 us
  waiting for transfers between devices  170 us (62%)
  matrix products  47.3 us (17%)
  local copies, waits for them, and re-layouts  23.9 us (9%)
  between operations  14.1 us (5%)
  other arithmetic  13.4 us (5%)
  starting transfers between devices  4.04 us (1%)
    reduce_scatter x1, waiting for transfers between devices, body(): lax.psum_scatter(term_maker(normed, targets), 'fsdp', scatter_dimension=0...  119 us
    ppermute x2, waiting for transfers between devices, body(): lax.ppermute(summed, 'rep', [(dev, dev ^ hop) for dev in range(4)])  50.7 us
    dot_general x1, matrix products, term_maker(): lax.dot_general(normed, part, (((0,), (0,)), ((), ())), preferred_element...  23.4 us
    div x2, local copies, waits for them, and re-layouts, body(): return (cleared[None], update / groups)  9.15 us
    dot_general x2, matrix products, body(): jnp.einsum('kn,akbl,lm->anbm', basis, summed, basis, precision=lax.Precis...  8.6 us
    dot_general x2, matrix products, settle(): jnp.einsum('kn,akbl,lm->anbm', basis, bands, basis, precision=lax.Precisi...  8.54 us
    reduce_sum x1, other arithmetic, body(): stat = jnp.mean(values * values, axis=-1, keepdims=True)  7.6 us
    dot_general x2, matrix products, bands_of(): jnp.einsum('kn,anbm,lm->akbl', basis, blocks, basis, precision=lax.Precis...  6.78 us
  transfers between devices with their start and end apart: 3, of which 3 were waited for; matrix products, arithmetic and copies ran while one was open for 6% of the time, Pallas kernels for 0%

profile of v1, /device:TPU:0, one launch (start us, length us, event | category | flops | bytes accessed | tf_op | source)
XLA Modules:
  0.0 272.4 jit_solution(1504084400739425403)
XLA Ops:
  7.2 0.0 reduce-scatter.2.cloned.1.call-start
  7.2 7.6 %fusion = f32[2048]{0:T(1024)S(1)} fusion(bf16[1,2048,4096]{2,1,0:T(8,128)(2,1)} %param.3), kind=kLoop, calls=%fused_computation.2 | loop fusion | flops 25163776 | bytes 16785408 | tf_op jit(solution)/shard_map/reduce_sum | solution.py:41
  14.8 3.1 %copy-done = bf16[1,2048,4096]{2,1,0:T(8,128)(2,1)S(1)} copy-done((bf16[1,2048,4096]{2,1,0:T(8,128)(2,1)S(1)}, bf16[1,2048,4096]{2,1,0:T(8,128)(2,1)}, u32[]{:S(2)}) %copy-start) | copy-done | bytes 16777240
  17.9 23.4 %fusion.3 = f32[4096,1024]{1,0:T(8,128)} fusion(bf16[1,2048,4096]{2,1,0:T(8,128)(2,1)S(1)} %copy-done, f32[2048]{0:T(1024)S(1)} %add_rsqrt_fusion, bf16[1,2048,1024]{2,1,0:T(8,128)(2,1)} %param.4), kind=kOutput, calls=%fused_computation.5 | convolution fusion | flops 17205035008 | bytes 37756928 | tf_op jit(solution)/shard_map/dot_general | solution.py:26
  41.3 0.0 reduce-scatter.2.cloned.1.call-update
  41.3 119.0 %reduce-scatter.2.cloned.1.call-done = f32[512,1024]{1,0:T(8,128)} async-done(((f32[4096,1024]{1,0:T(8,128)}), f32[512,1024]{1,0:T(8,128)}) %reduce-scatter.2.cloned.1.call-update) | async-done | bytes 2097168 | tf_op jit(solution)/shard_map/reduce_scatter | solution.py:46
  160.3 2.7 bitcast_add_fusion
  163.0 2.5 reshape.49
  165.5 5.8 %fusion.7 = f32[8,16,64,16]{2,3,1,0:T(8,128)S(1)} fusion(f32[8,64,16,64]{3,2,1,0:T(8,128)} %reshape.49, f32[16]{0:T(128)S(1)} %compare_select_fusion, f32[64]{0:T(128)S(1)} %add_multiply_fusion), kind=kOutput, calls=%fused_computation.8 | convolution fusion | flops 100666368 | bytes 2621760 | tf_op jit(solution)/shard_map/kn,anbm,lm->akbl/dot_general | solution.py:22
  171.3 1.0 convolution_bitcast_fusion.1
  172.3 1.8 fusion.14
  174.1 1.6 collective-permute-start
  175.7 6.7 %convolution_bitcast_fusion = f32[8,64,16,64]{3,1,2,0:T(8,128)S(1)} fusion(f32[8,16,16,64]{3,2,1,0:T(8,128)S(1)} %fusion.14, f32[16]{0:T(128)S(1)} %compare_select_fusion, f32[64]{0:T(128)S(1)} %add_multiply_fusion), kind=kOutput, calls=%fused_computation.11 | convolution fusion | flops 100666368 | bytes 2621760 | tf_op jit(solution)/shard_map/kn,akbl,lm->anbm/dot_general | solution.py:35
  182.4 4.3 %copy.6 = f32[8,64,16,64]{3,2,1,0:T(8,128)} copy(f32[8,64,16,64]{3,1,2,0:T(8,128)S(1)} %convolution_bitcast_fusion) | data formatting | bytes 4194304 | tf_op jit(solution)/shard_map/kn,akbl,lm->anbm/transpose | solution.py:35
  186.7 4.8 %reshape.50 = f32[512,1024]{1,0:T(8,128)} reshape(f32[8,64,16,64]{3,2,1,0:T(8,128)} %copy.6) | data formatting | bytes 4194304 | tf_op jit(solution)/shard_map/reshape | solution.py:36
  191.6 7.5 %collective-permute-done = f32[8,16,16,16]{3,1,2,0:T(8,128)} collective-permute-done((f32[8,16,16,16]{3,1,2,0:T(8,128)S(1)}, f32[8,16,16,16]{3,1,2,0:T(8,128)}, u32[]{:S(2)}, u32[]{:S(2)}) %collective-permute-start) | collective-permute-done | bytes 131104 | tf_op jit(solution)/shard_map/ppermute | solution.py:51
  199.1 1.4 add.48
  200.4 2.5 collective-permute-start.1
  202.9 1.7 subtract_bitcast_fusion
  204.6 43.2 %collective-permute-done.1 = f32[8,16,16,16]{3,1,2,0:T(8,128)S(1)} collective-permute-done((f32[8,16,16,16]{3,1,2,0:T(8,128)S(1)}, f32[8,16,16,16]{3,1,2,0:T(8,128)S(1)}, u32[]{:S(2)}, u32[]{:S(2)}) %collective-permute-start.1) | collective-permute-done | bytes 131104 | tf_op jit(solution)/shard_map/ppermute | solution.py:51
  247.7 1.8 fusion.9
  249.6 6.8 %multiply_bitcast_fusion = f32[8,64,16,64]{3,1,2,0:T(8,128)S(1)} fusion(f32[8,16,16,64]{3,2,1,0:T(8,128)S(1)} %fusion.9, f32[16]{0:T(128)S(1)} %compare_select_fusion, f32[64]{0:T(128)S(1)} %add_multiply_fusion), kind=kOutput, calls=%fused_computation.10 | convolution fusion | flops 101190656 | bytes 2621760 | tf_op jit(solution)/shard_map/kn,akbl,lm->anbm/dot_general | solution.py:52
  256.4 4.3 %copy.7 = f32[8,64,16,64]{3,2,1,0:T(8,128)} copy(f32[8,64,16,64]{3,1,2,0:T(8,128)S(1)} %multiply_bitcast_fusion) | data formatting | bytes 4194304 | tf_op jit(solution)/shard_map/div | solution.py:55
  260.7 4.8 %div.39 = f32[512,1024]{1,0:T(8,128)} reshape(f32[8,64,16,64]{3,2,1,0:T(8,128)} %copy.7) | data formatting | bytes 4194304 | tf_op jit(solution)/shard_map/div | solution.py:55
  (6 shorter events, 0.0 us)
Async XLA Ops:
  7.2 153.2 %reduce-scatter.2.cloned.1.call-start = ((), (), s32[]{:S(2)}) async-start(), calls=%async_computation.1 | async-start | bytes 18874368 | tf_op jit(solution)/shard_map/reduce_scatter | solution.py:46
  7.2 10.7 %copy-start = (bf16[1,2048,4096]{2,1,0:T(8,128)(2,1)S(1)}, bf16[1,2048,4096]{2,1,0:T(8,128)(2,1)}, u32[]{:S(2)}) copy-start(bf16[1,2048,4096]{2,1,0:T(8,128)(2,1)} %param.3) | copy-start | bytes 50331652
  174.1 24.9 %collective-permute-start = (f32[8,16,16,16]{3,1,2,0:T(8,128)S(1)}, f32[8,16,16,16]{3,1,2,0:T(8,128)}, u32[]{:S(2)}, u32[]{:S(2)}) collective-permute-start(f32[8,16,16,16]{3,1,2,0:T(8,128)S(1)} %convolution_bitcast_fusion.1), channel_id=1, source_target_pairs={{0,8},{8,0},{16,24},{24,16},{1,9},{9,1},{17,25},{25,17},{2,10},{10... | collective-permute-start | bytes 393224 | tf_op jit(solution)/shard_map/ppermute | solution.py:51
  191.6 11.3 %copy-start.1 = (f32[512,1024]{1,0:T(8,128)S(1)}, f32[512,1024]{1,0:T(8,128)}, u32[]{:S(2)}) copy-start(f32[512,1024]{1,0:T(8,128)} %reshape.50) | copy-start | bytes 6291460
  200.4 47.3 %collective-permute-start.1 = (f32[8,16,16,16]{3,1,2,0:T(8,128)S(1)}, f32[8,16,16,16]{3,1,2,0:T(8,128)S(1)}, u32[]{:S(2)}, u32[]{:S(2)}) collective-permute-start(f32[8,16,16,16]{3,1,2,0:T(8,128)S(1)} %add.48), channel_id=1, source_target_pairs={{0,16},{8,24},{16,0},{24,8},{1,17},{9,25},{17,1},{25,9},{2,18},{10... | collective-permute-start | bytes 393224 | tf_op jit(solution)/shard_map/ppermute | solution.py:51
Sparse Core Ops, SparseCore 0:
  41.4 118.8 reduce-scatter.1
